TPU v7x, 32 devices: a whole 2x2x4 slice. The times are simulated.
32 devices in a mesh: dp: 8 (over z, y), expert: 4 (over x, core).
Axes of the slice: x: 2, y: 2, z: 4, core: 2. Of those that a mesh axis runs over, the one named last changes fastest.
Arguments:
- tokens: bfloat16 [512, 2048], P(('dp', 'expert')), may hold values from -6 to 6
- expert_ids: int32 [512, 8], P(('dp', 'expert')), may hold values from 0 to 15, as said below
- route_weight: float32 [512, 8], P(('dp', 'expert')), may hold values from 0.03 to 0.6
- out_grad: bfloat16 [512, 2048], P(('dp', 'expert')), may hold values from -6 to 6
- gate_weight: bfloat16 [32, 2048, 384], P(('dp', 'expert')), may hold values from -0.125 to 0.125
- up_weight: bfloat16 [32, 2048, 384], P(('dp', 'expert')), may hold values from -0.125 to 0.125
- down_weight: bfloat16 [32, 384, 2048], P(('dp', 'expert')), may hold values from -0.21875 to 0.21875
Outputs:
- layer_out: bfloat16 [512, 2048], P(('dp', 'expert'))
- token_grad: bfloat16 [512, 2048], P(('dp', 'expert'))
- route_grad: float32 [512, 8], P(('dp', 'expert'))
- gate_grad: bfloat16 [32, 2048, 384], P(('dp', 'expert'))
- up_grad: bfloat16 [32, 2048, 384], P(('dp', 'expert'))
- down_grad: bfloat16 [32, 384, 2048], P(('dp', 'expert'))
Inputs may be any that keep to these rules, and one draw needn't show every extreme that they name: `expert_ids`: each row names 8 different experts. The rows of one device name no expert more than 16 times, and one expert is named exactly 16 times by the rows of every device.
All inputs are finite; a program needn't handle non-finite values.
Results may differ from a plain program's by a relative error of at most 0.0071.
Values may be sent and summed in bfloat16 or wider, within the bound.
A program may use at most 128 MiB of HBM per device.

v0:
```python
import jax
import jax.numpy as jnp
from jax import lax
from jax.sharding import PartitionSpec as P


def from_partner(shard, axis, apart):
    return lax.ppermute(shard, axis, [(i, i ^ 1 << apart) for i in range(lax.axis_size(axis))])


def contract(left_op, right_op, left_dim, right_dim):
    return lax.dot_general(
        left_op,
        right_op,
        (((left_dim,), (right_dim,)), ((), ())),
        preferred_element_type=jnp.float32,
    )


def deliver(buffer, dp_size, ex_size, experts, capacity, backward):
    feat_width = buffer.shape[1]
    doubled = jnp.broadcast_to(
        buffer.reshape(experts, 1, capacity, feat_width), (experts, 2, capacity, feat_width)
    )
    doubled = doubled.reshape(dp_size, ex_size, capacity, feat_width)
    if backward:
        arrived = lax.all_to_all(
            lax.all_to_all(doubled, "dp", split_axis=0, concat_axis=0, tiled=True),
            "expert",
            split_axis=1,
            concat_axis=1,
            tiled=True,
        )
    else:
        arrived = lax.all_to_all(
            lax.all_to_all(doubled, "dp", split_axis=0, concat_axis=0, tiled=True),
            "expert",
            split_axis=1,
            concat_axis=1,
            tiled=True,
        )
    return arrived.reshape(-1, feat_width)


def bring_back(partials_in, dp_size, ex_size, experts, capacity, half_index, backward):
    feat_width = partials_in.shape[1]
    if backward:
        partner = from_partner(partials_in, "expert", 0)
    else:
        partner = from_partner(partials_in, "expert", 0)
    summed = (partials_in.astype(jnp.float32) + partner.astype(jnp.float32)).astype(jnp.bfloat16)
    summed = summed.reshape(dp_size, ex_size, capacity, feat_width)
    own_half = lax.dynamic_slice_in_dim(summed, half_index * (capacity // 2), capacity // 2, 2)
    if backward:
        returned = lax.all_to_all(
            lax.all_to_all(own_half, "dp", split_axis=0, concat_axis=0, tiled=True),
            "expert",
            split_axis=1,
            concat_axis=1,
            tiled=True,
        )
    else:
        returned = lax.all_to_all(
            lax.all_to_all(own_half, "dp", split_axis=0, concat_axis=0, tiled=True),
            "expert",
            split_axis=1,
            concat_axis=1,
            tiled=True,
        )
    merged = returned.reshape(experts, capacity, feat_width)
    return merged.reshape(experts * capacity, feat_width)


AXES = ("dp", "expert")


def dense_body(tokens, expert_ids, route_weight, out_grad, gate_weight, up_weight, down_weight):
    pieces = lax.axis_size("dp") * lax.axis_size("expert")
    experts = pieces // 2
    tok_count, feat_width = tokens.shape
    mine = (lax.axis_index("dp") * lax.axis_size("expert") + lax.axis_index("expert")) // 2
    onehot = expert_ids[:, :, None] == jnp.arange(experts, dtype=jnp.int32)
    table = jnp.sum(jnp.where(onehot, route_weight[:, :, None], 0.0), axis=1)
    both = lax.all_gather(jnp.concatenate([tokens, out_grad], axis=1), AXES, axis=0, tiled=True)
    x_all, g_all = (both[:, :feat_width], both[:, feat_width:])
    weights = lax.all_gather(table, AXES, axis=0, tiled=True)
    weight = lax.dynamic_slice_in_dim(weights, mine, 1, 1)
    w_gate, w_up, w_down = (gate_weight[0], up_weight[0], down_weight[0])
    gate_act = contract(x_all, w_gate, 1, 0)
    up_act = contract(x_all, w_up, 1, 0)
    back = contract(g_all, w_down, 1, 1)
    sig = jax.nn.sigmoid(gate_act)
    hidden = gate_act * sig * up_act
    route = jnp.sum(hidden * back, axis=1)
    scaled_hidden = (weight * hidden).astype(jnp.bfloat16)
    back = weight * back
    gate_pre = (back * up_act * sig * (1.0 + gate_act * (1.0 - sig))).astype(jnp.bfloat16)
    up_pre = (back * gate_act * sig).astype(jnp.bfloat16)
    out_part = contract(scaled_hidden, w_down, 1, 0).astype(jnp.bfloat16)
    grad_part = (contract(gate_pre, w_gate, 1, 1) + contract(up_pre, w_up, 1, 1)).astype(
        jnp.bfloat16
    )
    gate_grad = contract(x_all, gate_pre, 0, 0).astype(jnp.bfloat16)
    up_grad = contract(x_all, up_pre, 0, 0).astype(jnp.bfloat16)
    down_grad = contract(scaled_hidden, g_all, 0, 0).astype(jnp.bfloat16)
    summed = lax.psum_scatter(
        jnp.concatenate([out_part, grad_part], axis=1), AXES, scatter_dimension=0, tiled=True
    )
    routes = lax.all_to_all(route.reshape(pieces, tok_count), AXES, 0, 0, tiled=True)
    routes = jnp.sum(routes.reshape(experts, 2, tok_count), axis=1)
    route_grad = jnp.sum(jnp.where(onehot, routes.T[:, None, :], 0.0), axis=2)
    return (
        summed[:, :feat_width],
        summed[:, feat_width:],
        route_grad,
        gate_grad[None],
        up_grad[None],
        down_grad[None],
    )


def body(tokens, expert_ids, route_weight, out_grad, gate_weight, up_weight, down_weight):
    dp_size = lax.axis_size("dp")
    ex_size = lax.axis_size("expert")
    tok_count, feat_width = tokens.shape
    top_count = expert_ids.shape[1]
    experts = dp_size * ex_size // 2
    assigned = tok_count * top_count
    capacity = 2 * (assigned // experts)
    half_index = lax.axis_index("expert") % 2
    flat_ids = expert_ids.reshape(-1)
    onehot = (flat_ids[:, None] == jnp.arange(experts, dtype=jnp.int32)[None, :]).astype(jnp.int32)
    before = jnp.cumsum(onehot, axis=0) - onehot
    slot_ids = jnp.sum(before * onehot, axis=1)
    place_row = flat_ids * capacity + slot_ids
    source = (
        jnp.full((experts * capacity,), -1, jnp.int32)
        .at[place_row]
        .set(jnp.arange(assigned, dtype=jnp.int32))
    )
    filled = source >= 0
    assign = jnp.maximum(source, 0)
    rows_tok = assign // top_count
    send_rows = jnp.where(filled[:, None], tokens[rows_tok], jnp.zeros((), jnp.bfloat16))
    in_rows = deliver(send_rows, dp_size, ex_size, experts, capacity, False)
    w_gate = gate_weight[0]
    w_up = up_weight[0]
    w_down = down_weight[0]
    gate_act = jnp.dot(in_rows, w_gate, preferred_element_type=jnp.float32)
    up_act = jnp.dot(in_rows, w_up, preferred_element_type=jnp.float32)
    sig_gate = jax.nn.sigmoid(gate_act)
    hidden = (gate_act * sig_gate * up_act).astype(jnp.bfloat16)
    partial_value = jnp.dot(hidden, w_down, preferred_element_type=jnp.float32).astype(jnp.bfloat16)
    expert_table = bring_back(partial_value, dp_size, ex_size, experts, capacity, half_index, False)
    expert_rows = expert_table[place_row].reshape(tok_count, top_count, feat_width)
    layer_out = jnp.sum(route_weight[:, :, None] * expert_rows.astype(jnp.float32), axis=1).astype(
        jnp.bfloat16
    )
    route_grad = jnp.einsum("tkd,td->tk", expert_rows, out_grad, preferred_element_type=jnp.float32)
    scaled = (route_weight[:, :, None] * out_grad[:, None, :].astype(jnp.float32)).astype(
        jnp.bfloat16
    )
    scaled = scaled.reshape(assigned, feat_width)
    send_grad = jnp.where(filled[:, None], scaled[assign], jnp.zeros((), jnp.bfloat16))
    grad_rows = deliver(send_grad, dp_size, ex_size, experts, capacity, True)
    hidden_grad = contract(grad_rows, w_down, 1, 1)
    gate_pre = (hidden_grad * up_act * sig_gate * (1.0 + gate_act * (1.0 - sig_gate))).astype(
        jnp.bfloat16
    )
    up_pre = (hidden_grad * gate_act * sig_gate).astype(jnp.bfloat16)
    partial_grad = (contract(gate_pre, w_gate, 1, 1) + contract(up_pre, w_up, 1, 1)).astype(
        jnp.bfloat16
    )
    gate_grad = contract(in_rows, gate_pre, 0, 0).astype(jnp.bfloat16)
    up_grad = contract(in_rows, up_pre, 0, 0).astype(jnp.bfloat16)
    down_grad = contract(hidden, grad_rows, 0, 0).astype(jnp.bfloat16)
    grad_table = bring_back(partial_grad, dp_size, ex_size, experts, capacity, half_index, True)
    expert_grad = grad_table[place_row].reshape(tok_count, top_count, feat_width)
    token_grad = jnp.sum(expert_grad.astype(jnp.float32), axis=1).astype(jnp.bfloat16)
    return (layer_out, token_grad, route_grad, gate_grad[None], up_grad[None], down_grad[None])


def solution(mesh):
    in_specs = (
        P(("dp", "expert"), None),
        P(("dp", "expert"), None),
        P(("dp", "expert"), None),
        P(("dp", "expert"), None),
        P(("dp", "expert"), None, None),
        P(("dp", "expert"), None, None),
        P(("dp", "expert"), None, None),
    )
    out_specs = (
        P(("dp", "expert"), None),
        P(("dp", "expert"), None),
        P(("dp", "expert"), None),
        P(("dp", "expert"), None, None),
        P(("dp", "expert"), None, None),
        P(("dp", "expert"), None, None),
    )
    pieces = mesh.shape["dp"] * mesh.shape["expert"]

    def step(tokens, expert_ids, *rest):
        capacity = 2 * (tokens.shape[0] * expert_ids.shape[1] // (pieces // 2))
        form = dense_body if capacity >= tokens.shape[0] else body
        return form(tokens, expert_ids, *rest)

    return jax.shard_map(step, mesh=mesh, in_specs=in_specs, out_specs=out_specs, check_vma=False)
```

profile of v0, /device:TPU:0, one launch (start us, length us, event | category | flops | bytes accessed | tf_op | source)
XLA Modules:
  0.0 291.6 jit_solution(5355917034021186230)
XLA Ops:
  7.2 0.0 all-gather.2.cloned.1.call-start
  7.2 1.6 pad_maximum_fusion.1
  8.9 0.0 all-gather.2.cloned.1.call-update
  8.9 67.0 %all-gather.2.cloned.1.call-done = bf16[512,4096]{1,0:T(8,128)(2,1)} async-done(((bf16[16,4096]{1,0:T(8,128)(2,1)}), bf16[512,4096]{1,0:T(8,128)(2,1)}) %all-gather.2.cloned.1.call-update) | async-done | bytes 4194320 | tf_op jit(solution)/shard_map/all_gather | solution.py:84
  75.9 3.1 %fusion.9 = f32[512,384]{0,1:T(8,128)S(1)} fusion(bf16[1,2048,384]{2,1,0:T(8,128)(2,1)} %param.12, bf16[512,4096]{1,0:T(8,128)(2,1)} %all-gather.2.cloned.1.call-done), kind=kOutput, calls=%fused_computation.15 | convolution fusion | flops 805306368 | bytes 4456448 | tf_op jit(solution)/shard_map/dot_general | solution.py:12
  79.0 2.9 %fusion.13 = f32[512,384]{0,1:T(8,128)S(1)} fusion(bf16[1,2048,384]{2,1,0:T(8,128)(2,1)S(1)} %copy-done.1, bf16[512,4096]{1,0:T(8,128)(2,1)} %all-gather.2.cloned.1.call-done), kind=kOutput, calls=%fused_computation.19 | convolution fusion | flops 805306368 | bytes 4456448 | tf_op jit(solution)/shard_map/dot_general | solution.py:12
  82.0 0.1 copy-done.12
  82.1 1.9 multiply_reduce_fusion
  84.1 0.7 all_to_all.6
  84.7 3.4 %all-to-all-start = ((f32[32,1,16]{2,1,0:T(1,128)}), f32[32,1,16]{2,1,0:T(1,128)S(1)}, u32[]{:S(2)}, u32[]{:S(2)}) async-start(f32[32,1,16]{2,1,0:T(1,128)} %bitcast.3), calls=%async_computation.1 | async-start | bytes 32768 | tf_op jit(solution)/shard_map/all_to_all | solution.py:109
  88.1 0.0 reduce-scatter.2.cloned.1.call-start
  88.2 0.1 copy.21
  88.3 0.1 copy.22
  88.4 6.9 %all-to-all-done = f32[32,1,16]{2,1,0:T(1,128)S(1)} async-done(((f32[32,1,16]{2,1,0:T(1,128)}), f32[32,1,16]{2,1,0:T(1,128)S(1)}, u32[]{:S(2)}, u32[]{:S(2)}) %all-to-all-start) | async-done | bytes 2080 | tf_op jit(solution)/shard_map/all_to_all | solution.py:109
  95.3 0.1 copy.24
  95.3 0.2 select_reduce_fusion
  95.5 37.6 %all_gather.6 = f32[512,16]{1,0:T(8,128)S(1)} all-gather(f32[16,16]{1,0:T(8,128)S(1)} %get-tuple-element.13), channel_id=1, replica_groups=mesh['dp'=8,'expert'=4] {'dp','expert'}, dimensions={0}, use_global_device_ids=true | all-gather | bytes 33792 | tf_op jit(solution)/shard_map/all_gather | solution.py:86
  133.1 0.2 dynamic-slice_reduce_fusion
  133.3 2.9 convolution_convert_fusion
  136.2 0.4 multiply_convert_fusion
  136.7 1.0 copy-done.2
  137.6 1.3 fusion.11
  138.9 0.1 copy-done.3
  139.0 1.4 add_convert_fusion
  140.4 2.5 pad_maximum_fusion
  142.9 0.0 reduce-scatter.2.cloned.1.call-update
  142.9 0.7 copy.25
  143.6 4.2 %fusion.1 = bf16[1,2048,384]{2,1,0:T(8,128)(2,1)} fusion(bf16[512,384]{0,1:T(8,128)(2,1)S(1)} %get-tuple-element.14, bf16[512,4096]{1,0:T(8,128)(2,1)} %all-gather.2.cloned.1.call-done), kind=kOutput, calls=%fused_computation.7 | convolution fusion | flops 806092800 | bytes 4063232 | tf_op jit(solution)/shard_map/dot_general | solution.py:12
  147.8 2.5 fusion
  150.2 2.2 fusion.2
  152.4 130.9 %reduce-scatter.2.cloned.1.call-done = bf16[16,4096]{1,0:T(8,128)(2,1)} async-done(((bf16[512,4096]{1,0:T(8,128)(2,1)}), bf16[16,4096]{1,0:T(8,128)(2,1)}) %reduce-scatter.2.cloned.1.call-update) | async-done | bytes 131088 | tf_op jit(solution)/shard_map/reduce_scatter | solution.py:106
  283.2 1.5 fusion.19
  (26 shorter events, 0.1 us)
Async XLA Ops:
  7.2 74.8 %copy-start = (bf16[1,384,2048]{2,1,0:T(8,128)(2,1)S(1)}, bf16[1,384,2048]{2,1,0:T(8,128)(2,1)}, u32[]{:S(2)}) copy-start(bf16[1,384,2048]{2,1,0:T(8,128)(2,1)} %param.13) | copy-start | bytes 4718596
  7.2 68.7 %all-gather.2.cloned.1.call-start = ((), (), s32[]{:S(2)}) async-start(), calls=%async_computation.2 | async-start | bytes 4325376 | tf_op jit(solution)/shard_map/all_gather | solution.py:84
  8.9 70.1 %copy-start.1 = (bf16[1,2048,384]{2,1,0:T(8,128)(2,1)S(1)}, bf16[1,2048,384]{2,1,0:T(8,128)(2,1)}, u32[]{:S(2)}) copy-start(bf16[1,2048,384]{2,1,0:T(8,128)(2,1)} %param.11) | copy-start | bytes 4718596
  79.0 3.0 %copy-start.4 = (f32[512,384]{0,1:T(8,128)}, f32[512,384]{0,1:T(8,128)S(1)}, u32[]{:S(2)}) copy-start(f32[512,384]{0,1:T(8,128)S(1)} %fusion.9) | copy-start | bytes 2359300
  79.0 3.1 %copy-start.12 = (bf16[512,4096]{1,0:T(8,128)(2,1)S(1)}, bf16[512,4096]{1,0:T(8,128)(2,1)}, u32[]{:S(2)}) copy-start(bf16[512,4096]{1,0:T(8,128)(2,1)} %all-gather.2.cloned.1.call-done) | copy-start | bytes 12582916
  82.1 2.0 copy-start.6
  82.1 6.1 %copy-start.10 = (s32[16,8]{0,1:T(8,128)S(1)}, s32[16,8]{0,1:T(8,128)}, u32[]{:S(2)}) copy-start(s32[16,8]{0,1:T(8,128)} %param.8) | copy-start | bytes 1540
  82.1 6.2 %copy-start.11 = (f32[16,8]{0,1:T(8,128)S(1)}, f32[16,8]{0,1:T(8,128)}, u32[]{:S(2)}) copy-start(f32[16,8]{0,1:T(8,128)} %param.9) | copy-start | bytes 1540
  84.7 10.5 %all-to-all-start = ((f32[32,1,16]{2,1,0:T(1,128)}), f32[32,1,16]{2,1,0:T(1,128)S(1)}, u32[]{:S(2)}, u32[]{:S(2)}) async-start(f32[32,1,16]{2,1,0:T(1,128)} %bitcast.3), calls=%async_computation.1 | async-start | bytes 32768 | tf_op jit(solution)/shard_map/all_to_all | solution.py:109
  88.1 195.1 %reduce-scatter.2.cloned.1.call-start = ((), (), s32[]{:S(2)}) async-start(), calls=%async_computation.3 | async-start | bytes 4325376 | tf_op jit(solution)/shard_map/reduce_scatter | solution.py:106
  133.3 2.9 %copy-start.5 = (f32[512,384]{0,1:T(8,128)S(1)}, f32[512,384]{0,1:T(8,128)}, u32[]{:S(2)}) copy-start(f32[512,384]{0,1:T(8,128)} %copy-done.4) | copy-start | bytes 2359300
  133.3 2.9 %copy-start.7 = (f32[512,384]{0,1:T(8,128)S(1)}, f32[512,384]{0,1:T(8,128)}, u32[]{:S(2)}) copy-start(f32[512,384]{0,1:T(8,128)} %copy-done.6) | copy-start | bytes 2359300
  133.3 2.9 %copy-start.9 = (f32[512,384]{0,1:T(8,128)S(1)}, f32[512,384]{0,1:T(8,128)}, u32[]{:S(2)}) copy-start(f32[512,384]{0,1:T(8,128)} %get-tuple-element.19) | copy-start | bytes 2359300
  136.2 1.4 copy-start.2
  137.6 1.4 copy-start.3
  143.6 4.2 %copy-start.13 = (bf16[512,4096]{1,0:T(8,128)(2,1)S(1)}, bf16[512,4096]{1,0:T(8,128)(2,1)}, u32[]{:S(2)}) copy-start(bf16[512,4096]{1,0:T(8,128)(2,1)} %all-gather.2.cloned.1.call-done) | copy-start | bytes 12582916
  147.7 2.5 copy-start.8
Sparse Core Ops, SparseCore 0:
  11.4 64.4 all-gather.1
  143.0 140.1 reduce-scatter.1
where the time goes:
time: 292 us
  waiting for transfers between devices  205 us (70%)
  blocking collectives  37.6 us (13%)
  matrix products  22.3 us (8%)
  between operations  14.2 us (5%)
  other arithmetic  4.72 us (2%)
  local copies, waits for them, and re-layouts  4.57 us (2%)
  starting transfers between devices  3.46 us (1%)
    reduce_scatter x1, waiting for transfers between devices, dense_body(): lax.psum_scatter(jnp.concatenate([out_part, grad_part], axis=1), AXES, sc...  131 us
    all_gather x1, waiting for transfers between devices, dense_body(): lax.all_gather(jnp.concatenate([tokens, out_grad], axis=1), AXES, axis=0,...  67 us
    all_gather x1, blocking collectives, dense_body(): weights = lax.all_gather(table, AXES, axis=0, tiled=True)  37.6 us
    dot_general x9, matrix products, contract(): lax.dot_general(left_op, right_op, (((left_dim,), (right_dim,)), ((), ())...  22.3 us
    all_to_all x1, waiting for transfers between devices, dense_body(): lax.all_to_all(route.reshape(pieces, tok_count), AXES, 0, 0, tiled=True)  6.88 us
  transfers between devices with their start and end apart: 3, of which 3 were waited for; matrix products, arithmetic and copies ran while one was open for 3% of the time, Pallas kernels for 0%

commit v1 on v0

--- a/solution.py
+++ b/solution.py
@@ -81,7 +81,15 @@
     mine = (lax.axis_index("dp") * lax.axis_size("expert") + lax.axis_index("expert")) // 2
     onehot = expert_ids[:, :, None] == jnp.arange(experts, dtype=jnp.int32)
     table = jnp.sum(jnp.where(onehot, route_weight[:, :, None], 0.0), axis=1)
-    both = lax.all_gather(jnp.concatenate([tokens, out_grad], axis=1), AXES, axis=0, tiled=True)
+    x = jnp.concatenate([tokens, out_grad], axis=1)
+    ways, here = (lax.axis_size(AXES), lax.axis_index(AXES))
+    both, reach = (x, 1)
+    while reach < ways:
+        theirs = lax.ppermute(both, AXES, [(d, d ^ reach) for d in range(ways)])
+        mine_first = jnp.concatenate([both, theirs], axis=0)
+        theirs_first = jnp.concatenate([theirs, both], axis=0)
+        both = jnp.where(here & reach == 0, mine_first, theirs_first)
+        reach = 2 * reach
     x_all, g_all = (both[:, :feat_width], both[:, feat_width:])
     weights = lax.all_gather(table, AXES, axis=0, tiled=True)
     weight = lax.dynamic_slice_in_dim(weights, mine, 1, 1)

time: 292 us -> 373 us (1.28)
  waiting for transfers between devices: 205 us -> 269 us
  starting transfers between devices: 3.46 us -> 14.3 us
  other arithmetic: 4.72 us -> 13.9 us
  matrix products: 22.3 us -> 16.9 us
    ppermute x0 -> x5, waiting for transfers between devices: none -> 131 us  [dense_body(): theirs = lax.ppermute(both, AXES, [(d, d ^ reach) for d in range(ways)])]
    all_gather x1 -> x0, waiting for transfers between devices: 67 us -> none  [dense_body(): lax.all_gather(jnp.concatenate([tokens, out_grad], axis=1), AXES, axis=0,...]
    select_n x0 -> x5, other arithmetic: none -> 9.62 us  [dense_body(): both = jnp.where(here & reach == 0, mine_first, theirs_first)]
    ppermute x0 -> x5, starting transfers between devices: none -> 9.12 us  [dense_body(): theirs = lax.ppermute(both, AXES, [(d, d ^ reach) for d in range(ways)])]
    dot_general x9, matrix products: 22.3 us -> 16.9 us  [contract(): lax.dot_general(left_op, right_op, (((left_dim,), (right_dim,)), ((), ())...]
  transfers between devices with their start and end apart: 3 -> 7, of which waited for: 3 -> 7; matrix products, arithmetic and copies ran while one was open for 3% -> 3% of each run, Pallas kernels for 0% -> 0%
where the time goes in v1:
time: 373 us; the launch traced here: 372 us
  waiting for transfers between devices  269 us (72%)
  blocking collectives  37.7 us (10%)
  matrix products  16.9 us (5%)
  starting transfers between devices  14.3 us (4%)
  between operations  14.3 us (4%)
  other arithmetic  13.9 us (4%)
  local copies, waits for them, and re-layouts  6.81 us (2%)
    ppermute x5, waiting for transfers between devices, dense_body(): theirs = lax.ppermute(both, AXES, [(d, d ^ reach) for d in range(ways)])  131 us
    reduce_scatter x1, waiting for transfers between devices, dense_body(): lax.psum_scatter(jnp.concatenate([out_part, grad_part], axis=1), AXES, sc...  131 us
    all_gather x1, blocking collectives, dense_body(): weights = lax.all_gather(table, AXES, axis=0, tiled=True)  37.7 us
    dot_general x9, matrix products, contract(): lax.dot_general(left_op, right_op, (((left_dim,), (right_dim,)), ((), ())...  16.9 us
    select_n x5, other arithmetic, dense_body(): both = jnp.where(here & reach == 0, mine_first, theirs_first)  9.62 us
    ppermute x5, starting transfers between devices, dense_body(): theirs = lax.ppermute(both, AXES, [(d, d ^ reach) for d in range(ways)])  9.12 us
  transfers between devices with their start and end apart: 7, of which 7 were waited for; matrix products, arithmetic and copies ran while one was open for 3% of the time, Pallas kernels for 0%

profile of v1, /device:TPU:0, one launch (start us, length us, event | category | flops | bytes accessed | tf_op | source)
XLA Modules:
  0.0 372.5 jit_solution(2702397746347863197)
XLA Ops:
  7.2 1.0 constant_dynamic-update-slice_fusion.1
  8.1 0.8 constant_dynamic-update-slice_fusion
  9.5 1.0 collective-permute-done
  10.5 2.9 collective-permute-start.1
  13.4 6.6 %collective-permute-done.1 = bf16[32,4096]{1,0:T(8,128)(2,1)S(1)} collective-permute-done((bf16[32,4096]{1,0:T(8,128)(2,1)S(1)}, bf16[32,4096]{1,0:T(8,128)(2,1)S(1)}, u32[]{:S(2)}, u32[]{:S(2)}) %collective-permute-start.1) | collective-permute-done | bytes 262176 | tf_op jit(solution)/shard_map/ppermute | solution.py:88
  20.1 1.8 collective-permute-start.2
  22.0 11.7 %collective-permute-done.2 = bf16[64,4096]{1,0:T(8,128)(2,1)} collective-permute-done((bf16[64,4096]{1,0:T(8,128)(2,1)S(1)}, bf16[64,4096]{1,0:T(8,128)(2,1)}, u32[]{:S(2)}, u32[]{:S(2)}) %collective-permute-start.2) | collective-permute-done | bytes 524320 | tf_op jit(solution)/shard_map/ppermute | solution.py:88
  33.7 1.5 maximum_select_fusion.2
  35.2 1.6 collective-permute-start.3
  36.8 22.3 %collective-permute-done.3 = bf16[128,4096]{1,0:T(8,128)(2,1)} collective-permute-done((bf16[128,4096]{1,0:T(8,128)(2,1)S(1)}, bf16[128,4096]{1,0:T(8,128)(2,1)}, u32[]{:S(2)}, u32[]{:S(2)}) %collective-permute-start.3) | collective-permute-done | bytes 1048608 | tf_op jit(solution)/shard_map/ppermute | solution.py:88
  59.1 3.6 maximum_select_fusion.1
  62.7 2.3 collective-permute-start.4
  65.0 89.3 %collective-permute-done.4 = bf16[256,4096]{1,0:T(8,128)(2,1)} collective-permute-done((bf16[256,4096]{1,0:T(8,128)(2,1)}, bf16[256,4096]{1,0:T(8,128)(2,1)}, u32[]{:S(2)}, u32[]{:S(2)}) %collective-permute-start.4) | collective-permute-done | bytes 2097184 | tf_op jit(solution)/shard_map/ppermute | solution.py:88
  154.3 4.4 %maximum_select_fusion = bf16[512,4096]{1,0:T(8,128)(2,1)S(1)} fusion(bf16[256,4096]{1,0:T(8,128)(2,1)} %collective-permute-done.4, bf16[256,4096]{1,0:T(8,128)(2,1)} %maximum_select_fusion.1, pred[]{:T(512)S(6)} %eq.31), kind=kLoop, calls=%fused_computation | loop fusion | flops 18874368 | bytes 8388609 | tf_op jit(solution)/shard_map/jit(_where)/select_n | solution.py:91
  158.7 1.0 fusion.9
  159.8 1.5 copy-done.3
  161.3 1.0 fusion.13
  162.4 2.0 multiply_reduce_fusion
  164.4 0.7 all_to_all.6
  165.1 5.1 %all-to-all-start = ((f32[32,1,16]{2,1,0:T(1,128)}), f32[32,1,16]{2,1,0:T(1,128)S(1)}, u32[]{:S(2)}, u32[]{:S(2)}) async-start(f32[32,1,16]{2,1,0:T(1,128)} %bitcast.3), calls=%async_computation.1 | async-start | bytes 32768 | tf_op jit(solution)/shard_map/all_to_all | solution.py:117
  170.5 6.9 %all-to-all-done = f32[32,1,16]{2,1,0:T(1,128)S(1)} async-done(((f32[32,1,16]{2,1,0:T(1,128)}), f32[32,1,16]{2,1,0:T(1,128)S(1)}, u32[]{:S(2)}, u32[]{:S(2)}) %all-to-all-start) | async-done | bytes 2080 | tf_op jit(solution)/shard_map/all_to_all | solution.py:117
  177.6 37.7 %all_gather.3 = f32[512,16]{1,0:T(8,128)S(1)} all-gather(f32[16,16]{1,0:T(8,128)S(1)} %get-tuple-element.13), channel_id=1, replica_groups=mesh['dp'=8,'expert'=4] {'dp','expert'}, dimensions={0}, use_global_device_ids=true | all-gather | bytes 33792 | tf_op jit(solution)/shard_map/all_gather | solution.py:94
  215.6 1.3 convolution_convert_fusion
  217.0 1.6 multiply_convert_fusion
  218.6 1.3 fusion.11
  220.0 1.4 add_convert_fusion
  221.4 2.4 pad_maximum_fusion
  224.5 4.2 %fusion.1 = bf16[1,2048,384]{2,1,0:T(8,128)(2,1)} fusion(bf16[512,384]{0,1:T(8,128)(2,1)S(1)} %get-tuple-element.14, bf16[512,4096]{1,0:T(8,128)(2,1)} %copy-done.1), kind=kOutput, calls=%fused_computation.8 | convolution fusion | flops 806092800 | bytes 4063232 | tf_op jit(solution)/shard_map/dot_general | solution.py:12
  228.7 2.5 fusion
  231.2 2.2 fusion.2
  233.4 130.7 %reduce-scatter.2.cloned.1.call-done = bf16[16,4096]{1,0:T(8,128)(2,1)} async-done(((bf16[512,4096]{1,0:T(8,128)(2,1)}), bf16[16,4096]{1,0:T(8,128)(2,1)}) %reduce-scatter.2.cloned.1.call-update) | async-done | bytes 131088 | tf_op jit(solution)/shard_map/reduce_scatter | solution.py:114
  364.1 1.5 fusion.19
  (35 shorter events, 2.1 us)
Async XLA Ops:
  7.2 155.2 %copy-start = (bf16[1,384,2048]{2,1,0:T(8,128)(2,1)S(1)}, bf16[1,384,2048]{2,1,0:T(8,128)(2,1)}, u32[]{:S(2)}) copy-start(bf16[1,384,2048]{2,1,0:T(8,128)(2,1)} %param.13) | copy-start | bytes 4718596
  9.0 1.5 collective-permute-start
  10.5 9.5 %collective-permute-start.1 = (bf16[32,4096]{1,0:T(8,128)(2,1)S(1)}, bf16[32,4096]{1,0:T(8,128)(2,1)S(1)}, u32[]{:S(2)}, u32[]{:S(2)}) collective-permute-start(bf16[32,4096]{1,0:T(8,128)(2,1)S(1)} %maximum_select_fusion.4), channel_id=1, source_target_pairs={{0,2},{1,3},{2,0},{3,1},{4,6},{5,7},{6,4},{7,5},{8,10},{9,11},{10,... | collective-permute-start | bytes 786440 | tf_op jit(solution)/shard_map/ppermute | solution.py:88
  20.1 13.6 %collective-permute-start.2 = (bf16[64,4096]{1,0:T(8,128)(2,1)S(1)}, bf16[64,4096]{1,0:T(8,128)(2,1)}, u32[]{:S(2)}, u32[]{:S(2)}) collective-permute-start(bf16[64,4096]{1,0:T(8,128)(2,1)S(1)} %maximum_select_fusion.3), channel_id=1, source_target_pairs={{0,4},{1,5},{2,6},{3,7},{4,0},{5,1},{6,2},{7,3},{8,12},{9,13},{10,... | collective-permute-start | bytes 1572872 | tf_op jit(solution)/shard_map/ppermute | solution.py:88
  35.2 24.0 %collective-permute-start.3 = (bf16[128,4096]{1,0:T(8,128)(2,1)S(1)}, bf16[128,4096]{1,0:T(8,128)(2,1)}, u32[]{:S(2)}, u32[]{:S(2)}) collective-permute-start(bf16[128,4096]{1,0:T(8,128)(2,1)S(1)} %maximum_select_fusion.2), channel_id=1, source_target_pairs={{0,8},{1,9},{2,10},{3,11},{4,12},{5,13},{6,14},{7,15},{8,0},{9,1},... | collective-permute-start | bytes 3145736 | tf_op jit(solution)/shard_map/ppermute | solution.py:88
  62.7 91.6 %collective-permute-start.4 = (bf16[256,4096]{1,0:T(8,128)(2,1)}, bf16[256,4096]{1,0:T(8,128)(2,1)}, u32[]{:S(2)}, u32[]{:S(2)}) collective-permute-start(bf16[256,4096]{1,0:T(8,128)(2,1)} %maximum_select_fusion.1), channel_id=1, source_target_pairs={{0,16},{1,17},{2,18},{3,19},{4,20},{5,21},{6,22},{7,23},{8,24},{9,... | collective-permute-start | bytes 6291464 | tf_op jit(solution)/shard_map/ppermute | solution.py:88
  65.0 93.7 %copy-start.5 = (bf16[1,2048,384]{2,1,0:T(8,128)(2,1)S(1)}, bf16[1,2048,384]{2,1,0:T(8,128)(2,1)}, u32[]{:S(2)}) copy-start(bf16[1,2048,384]{2,1,0:T(8,128)(2,1)} %param.12) | copy-start | bytes 4718596
  158.7 3.6 copy-start.1
  158.7 2.6 copy-start.3
  162.4 53.2 %copy-start.7 = (f32[512,384]{0,1:T(8,128)}, f32[512,384]{0,1:T(8,128)S(1)}, u32[]{:S(2)}) copy-start(f32[512,384]{0,1:T(8,128)S(1)} %fusion.13) | copy-start | bytes 2359300
  162.4 7.9 %copy-start.10 = (s32[16,8]{0,1:T(8,128)S(1)}, s32[16,8]{0,1:T(8,128)}, u32[]{:S(2)}) copy-start(s32[16,8]{0,1:T(8,128)} %param.8) | copy-start | bytes 1540
  162.4 8.0 %copy-start.11 = (f32[16,8]{0,1:T(8,128)S(1)}, f32[16,8]{0,1:T(8,128)}, u32[]{:S(2)}) copy-start(f32[16,8]{0,1:T(8,128)} %param.9) | copy-start | bytes 1540
  165.1 12.3 %all-to-all-start = ((f32[32,1,16]{2,1,0:T(1,128)}), f32[32,1,16]{2,1,0:T(1,128)S(1)}, u32[]{:S(2)}, u32[]{:S(2)}) async-start(f32[32,1,16]{2,1,0:T(1,128)} %bitcast.3), calls=%async_computation.1 | async-start | bytes 32768 | tf_op jit(solution)/shard_map/all_to_all | solution.py:117
  170.3 193.8 %reduce-scatter.2.cloned.1.call-start = ((), (), s32[]{:S(2)}) async-start(), calls=%async_computation.2 | async-start | bytes 4325376 | tf_op jit(solution)/shard_map/reduce_scatter | solution.py:114
  215.6 1.4 copy-start.9
  217.0 1.7 copy-start.4
  218.6 1.4 copy-start.6
  224.5 4.2 %copy-start.2 = (bf16[512,4096]{1,0:T(8,128)(2,1)S(1)}, bf16[512,4096]{1,0:T(8,128)(2,1)}, u32[]{:S(2)}) copy-start(bf16[512,4096]{1,0:T(8,128)(2,1)} %copy-done.1) | copy-start | bytes 12582916
  228.7 2.5 copy-start.8
Sparse Core Ops, SparseCore 0:
  224.0 140.0 reduce-scatter.1
